TPU v7x, 256 devices: a whole 4x4x8 slice. The times are simulated.
256 devices in a mesh: row: 16 (over x, y_lo, core), col: 16 (over y_hi, z).
Axes of the slice: x: 4, y: 4 (y_hi: 2, y_lo: 2; y = y_hi * 2 + y_lo), z: 8, core: 2. Of those that a mesh axis runs over, the one named last changes fastest.
Arguments:
- blocks: bfloat16 [16, 16, 256, 128, 128], P('row', 'col'), may hold values from -0.0234375 to 0.0234375
- block_rows: int32 [16, 16, 256], P('row', 'col'), may hold values from 0 to 31, as said below
- block_cols: int32 [16, 16, 256], P('row', 'col'), may hold values from 0 to 31, as said below
- block_count: int32 [16, 16], P('row', 'col'), may hold values from 64 to 256, as said below
- probes: float32 [64, 65536], P(None, ('row', 'col')), may hold values from -6 to 6
- t_prev: float32 [64, 65536], P(None, ('row', 'col')), may hold values from -6 to 6
- t_cur: float32 [64, 65536], P(None, ('row', 'col')), may hold values from -6 to 6
- accum: float32 [64, 65536], P(None, ('row', 'col')), may hold values from -6 to 6
- coeffs: float32 [2], replicated, may hold values from 0.5 to 1.5
Outputs:
- t_next: float32 [64, 65536], P(None, ('row', 'col'))
- t_after: float32 [64, 65536], P(None, ('row', 'col'))
- accum_out: float32 [64, 65536], P(None, ('row', 'col'))
- moments: float32 [2, 64], replicated
Inputs may be any that keep to these rules, and one draw needn't show every extreme that they name: `block_rows`: within one device the live slots name distinct blocks; block rows lie in [0, 32) and block columns in [0, 32). `block_cols`: pairs with block_rows: within one device the live slots name distinct blocks. `block_count`: some device has all 256 slots live in every draw.
All inputs are finite; a program needn't handle non-finite values.
Results may differ from a plain program's by a relative error of at most 0.0025.
Values may be sent and summed in bfloat16 or wider, within the bound.
A program may use at most 64 MiB of HBM per device.

v0:
```python
import jax
import jax.numpy as jnp
from jax import lax
from jax.sharding import PartitionSpec as P


def local(blocks, block_rows, block_cols, block_count, probes, t_prev, t_cur, accum, coeffs):
    tiles_all = blocks[0, 0]
    row_ids = block_rows[0, 0]
    col_ids = block_cols[0, 0]
    live_total = block_count[0, 0]
    slot_total = tiles_all.shape[0]
    tile_size = tiles_all.shape[-1]
    probe_count = t_cur.shape[0]
    width = t_cur.shape[1]
    local_rows = width // tile_size * lax.axis_size("col")
    group_size = min(32, slot_total)
    turns = (live_total + group_size - 1) // group_size
    total_rows = width * lax.axis_size("row") * lax.axis_size("col")

    def product(vectors):
        gathered = lax.all_gather(vectors.astype(jnp.bfloat16), "row", axis=1, tiled=True)
        column_set = gathered.reshape(probe_count, -1, tile_size)

        def add_group(step_idx, total):
            first_slot = jnp.minimum(step_idx * group_size, slot_total - group_size)
            tile_group = lax.dynamic_slice_in_dim(tiles_all, first_slot, group_size, 0)
            group_rows = lax.dynamic_slice_in_dim(row_ids, first_slot, group_size, 0)
            group_cols = lax.dynamic_slice_in_dim(col_ids, first_slot, group_size, 0)
            slot_ids = first_slot + jnp.arange(group_size, dtype=jnp.int32)
            alive = (slot_ids >= step_idx * group_size) & (slot_ids < live_total)
            picked = jnp.take(column_set, group_cols, axis=1)
            contrib = jnp.einsum(
                "pgj,gij->pgi", picked, tile_group, preferred_element_type=jnp.float32
            )
            contrib = jnp.where(alive[None, :, None], contrib, 0.0)
            return total.at[:, group_rows, :].add(contrib)

        start = jnp.zeros((probe_count, local_rows, tile_size), jnp.float32)
        partial_value = lax.fori_loop(0, turns, add_group, start).reshape(
            probe_count, local_rows * tile_size
        )
        summed = lax.psum(partial_value, "col")
        return lax.dynamic_slice_in_dim(summed, lax.axis_index("col") * width, width, 1)

    def moment_one(local_sum):
        return lax.psum(local_sum, ("row", "col"))

    scale = float(total_rows) ** (-0.5)
    t_next = 2.0 * product(t_cur) - t_prev
    local_first = jnp.sum(probes * t_next, axis=1)
    first = moment_one(local_first)
    t_after = 2.0 * product(t_next) - t_cur
    second = moment_one(jnp.sum(probes * t_after, axis=1))
    moments = jnp.stack([first, second]) * scale
    accum_out = accum + coeffs[0] * t_next + coeffs[1] * t_after
    return (t_next, t_after, accum_out, moments)


def solution(mesh):
    return jax.shard_map(
        local,
        mesh=mesh,
        in_specs=(
            P("row", "col", None, None, None),
            P("row", "col", None),
            P("row", "col", None),
            P("row", "col"),
            P(None, ("row", "col")),
            P(None, ("row", "col")),
            P(None, ("row", "col")),
            P(None, ("row", "col")),
            P(),
        ),
        out_specs=(P(None, ("row", "col")), P(None, ("row", "col")), P(None, ("row", "col")), P()),
        check_vma=False,
    )
```

profile of v0, /device:TPU:1, one launch (start us, length us, event | category | flops | bytes accessed | tf_op | source)
XLA Modules:
  0.0 565.4 jit_solution(14219465716879633594)
XLA Ops:
  8.7 22.4 %all_gather.6 = bf16[64,4096]{1,0:T(8,128)(2,1)S(1)} all-gather(bf16[64,256]{1,0:T(8,128)(2,1)S(1)} %convert_element_type.6), channel_id=1, replica_groups=mesh['row'=16,'col'=16] {'row'}, dimensions={1}, use_global_device_ids=true | all-gather | bytes 557056 | tf_op jit(solution)/shard_map/all_gather | solution.py:22
  31.4 28.3 %while.20 = (s32[]{:T(128)}, f32[64,32,128]{2,0,1:T(8,128)S(1)}, s32[]{:T(128)}, s32[256]{0:T(256)}, s32[]{:T(128)}, /*index=5*/bf16[256,128,128]{2,1,0:T(8,128)...) while((s32[]{:T(128)}, f32[64,32,128]{2,0,1:T(8,128)S(1)}, ...), condition=%wide.region_2.4_spmd, body=%wide.region_0.3_spmd.sunk | while | flops 67896744 | bytes 6821079 | solution.py:40
  32.2 1.4 compare_and_fusion.6
  34.3 2.1 fusion.30
  36.4 2.1 scatter_fusion
  39.3 1.4 compare_and_fusion.6
  41.4 2.1 fusion.30
  43.4 2.1 scatter_fusion
  46.4 1.4 compare_and_fusion.6
  48.4 2.1 fusion.30
  50.5 2.1 scatter_fusion
  53.4 1.4 compare_and_fusion.6
  55.5 2.1 fusion.30
  57.6 2.1 scatter_fusion
  60.9 175.2 %all-reduce.4.cloned.1.call-done = f32[64,4096]{1,0:T(8,128)} async-done(((f32[64,4096]{1,0:T(8,128)}), f32[64,4096]{1,0:T(8,128)}) %all-reduce.4.cloned.1.call-update) | async-done | bytes 1048592 | tf_op jit(solution)/shard_map/psum | solution.py:43
  237.0 31.4 %all_gather.7 = bf16[64,4096]{1,0:T(8,128)(2,1)S(1)} all-gather(bf16[64,256]{1,0:T(8,128)(2,1)S(1)} %get-tuple-element.158), channel_id=1, replica_groups=mesh['row'=16,'col'=16] {'row'}, dimensions={1}, use_global_device_ids=true | all-gather | bytes 557056 | tf_op jit(solution)/shard_map/all_gather | solution.py:22
  268.7 28.3 %while.21 = (s32[]{:T(128)}, f32[64,32,128]{2,0,1:T(8,128)S(1)}, s32[]{:T(128)}, s32[256]{0:T(256)}, s32[]{:T(128)}, /*index=5*/bf16[256,128,128]{2,1,0:T(8,128)...) while((s32[]{:T(128)}, f32[64,32,128]{2,0,1:T(8,128)S(1)}, ...), condition=%wide.region_6.8_spmd, body=%wide.region_4.7_spmd.sunk | while | flops 67896744 | bytes 6821079 | solution.py:40
  269.5 1.4 compare_and_fusion.7
  271.6 2.1 fusion.33
  273.7 2.1 scatter_fusion.1
  276.6 1.4 compare_and_fusion.7
  278.7 2.1 fusion.33
  280.8 2.1 scatter_fusion.1
  283.7 1.4 compare_and_fusion.7
  285.7 2.1 fusion.33
  287.8 2.1 scatter_fusion.1
  290.7 1.4 compare_and_fusion.7
  292.8 2.1 fusion.33
  294.9 2.1 scatter_fusion.1
  298.8 171.2 %all-reduce.6.cloned.1.call-done = f32[64,4096]{1,0:T(8,128)} async-done(((f32[64,4096]{1,0:T(8,128)}), f32[64,4096]{1,0:T(8,128)}) %all-reduce.6.cloned.1.call-update) | async-done | bytes 1048592 | tf_op jit(solution)/shard_map/psum | solution.py:43
  470.9 85.2 %all-reduce = (f32[1,64]{1,0:T(1,128)S(1)}, f32[1,64]{1,0:T(1,128)S(1)}) all-reduce(f32[1,64]{1,0:T(1,128)S(1)} %bitcast.50, f32[1,64]{1,0:T(1,128)S(1)} %bitcast.49), channel_id=1, replica_groups=mesh['row'=16,'col'=16] {'row','col'}, use_global_device_ids=true, to_apply=%region_11.13 | all-reduce | flops 128 | bytes 1024 | tf_op jit(solution)/shard_map/psum | solution.py:47
  556.7 1.9 multiply_add_fusion
  (53 shorter events, 18.0 us)
Async XLA Ops:
  7.2 228.9 %all-reduce.4.cloned.1.call-start = ((), (), s32[]{:S(2)}) async-start(), calls=%async_computation | async-start | bytes 2097152 | tf_op jit(solution)/shard_map/psum | solution.py:43
  31.4 204.7 %copy-start.3 = (f32[64,256]{1,0:T(8,128)S(1)}, f32[64,256]{1,0:T(8,128)}, u32[]{:S(2)}) copy-start(f32[64,256]{1,0:T(8,128)} %param.20) | copy-start | bytes 196612
  60.8 409.1 %all-reduce.6.cloned.1.call-start = ((), (), s32[]{:S(2)}) async-start(), calls=%async_computation.1 | async-start | bytes 2097152 | tf_op jit(solution)/shard_map/psum | solution.py:43
  236.9 319.8 %copy-start = (f32[64,256]{1,0:T(8,128)}, f32[64,256]{1,0:T(8,128)S(1)}, u32[]{:S(2)}) copy-start(f32[64,256]{1,0:T(8,128)S(1)} %get-tuple-element.159) | copy-start | bytes 196612
  268.7 29.5 %copy-start.6 = (f32[2]{0:T(128)S(1)}, f32[2]{0:T(128)}, u32[]{:S(2)}) copy-start(f32[2]{0:T(128)} %param.23) | copy-start | bytes 28
  268.7 201.3 %copy-start.1 = (f32[64,256]{1,0:T(8,128)S(1)}, f32[64,256]{1,0:T(8,128)}, u32[]{:S(2)}) copy-start(f32[64,256]{1,0:T(8,128)} %param.21) | copy-start | bytes 196612
  268.7 201.3 %copy-start.4 = (f32[64,256]{1,0:T(8,128)S(1)}, f32[64,256]{1,0:T(8,128)}, u32[]{:S(2)}) copy-start(f32[64,256]{1,0:T(8,128)} %param.19) | copy-start | bytes 196612
  268.7 288.0 %copy-start.5 = (f32[64,256]{1,0:T(8,128)S(1)}, f32[64,256]{1,0:T(8,128)}, u32[]{:S(2)}) copy-start(f32[64,256]{1,0:T(8,128)} %param.22) | copy-start | bytes 196612
  470.9 87.7 %copy-start.2 = (f32[64,256]{1,0:T(8,128)}, f32[64,256]{1,0:T(8,128)S(1)}, u32[]{:S(2)}) copy-start(f32[64,256]{1,0:T(8,128)S(1)} %get-tuple-element.157) | copy-start | bytes 196612
Sparse Core Ops, SparseCore 0:
  61.0 175.0 all-reduce.3
  298.3 171.6 all-reduce.5
where the time goes:
time: 567 us; the launch traced here: 565 us
  waiting for transfers between devices  346 us (61%)
  blocking collectives  139 us (25%)
  other arithmetic  39.5 us (7%)
  matrix products  16.6 us (3%)
  between operations  14.8 us (3%)
  local copies, waits for them, and re-layouts  8.5 us (1%)
    psum x2, waiting for transfers between devices, product(): summed = lax.psum(partial_value, 'col')  346 us
    psum x1, blocking collectives, moment_one(): return lax.psum(local_sum, ('row', 'col'))  85.2 us
    all_gather x2, blocking collectives, product(): lax.all_gather(vectors.astype(jnp.bfloat16), 'row', axis=1, tiled=True)  53.9 us
    scatter-add x8, other arithmetic, add_group(): return total.at[:, group_rows, :].add(contrib)  17 us
    dot_general x8, matrix products, add_group(): jnp.einsum('pgj,gij->pgi', picked, tile_group, preferred_element_type=jnp...  16.6 us
  transfers between devices with their start and end apart: 2, of which 2 were waited for; matrix products, arithmetic and copies ran while one was open for 0% of the time, Pallas kernels for 0%

commit v1 on v0

v1 whole, which is shorter than its diff:
```python
import jax
import jax.numpy as jnp
from jax import lax
from jax.experimental import pallas as pl
from jax.experimental.pallas import tpu as pltpu
from jax.sharding import PartitionSpec as P

MESH = pl.DeviceIdType.MESH
F32 = jnp.float32
BF16 = jnp.bfloat16
BS = 128
PROBES = 64
MAXB = 256
LROWS = 32
PAIRS = 144
TAB = 384
UNROLL = 24
ROW_OFFS = ((2, 1), (2, 0), (1, 1), (3, 1), (1, 0), (3, 0), (0, 1))
COL_OFFS = (
    (1, 4), (0, 4), (1, 3), (1, 5), (0, 3), (0, 5), (1, 2), (1, 6),
    (0, 2), (0, 6), (1, 1), (1, 7), (0, 1), (0, 7), (1, 0),
)


def iota(shape, axis):
    return lax.broadcasted_iota(jnp.int32, shape, axis)


def to_sub(row):
    n = row.shape[1]
    eye = iota((n, n), 0) == iota((n, n), 1)
    return jnp.sum(jnp.where(eye, row, 0), axis=1, keepdims=True)


def tables(rows, cols, count):
    total = lambda mask, value, axis: jnp.sum(jnp.where(mask, value, 0), axis=axis, keepdims=True)
    live = iota((1, MAXB), 1) < count
    row_l = jnp.where(live, rows, 1000)
    row_c, col_c = to_sub(row_l), to_sub(cols)
    rho = total((row_c == row_l) & (col_c < cols), 1, 0)
    hit = iota((LROWS, MAXB), 0) == row_l
    pairs_c = (total(hit, 1, 1) + 1) >> 1
    i0, i1 = iota((LROWS, BS), 0), iota((LROWS, BS), 1)
    base_l = total(i0 < i1, pairs_c, 0)
    pairs_l = total(i0 == i1, pairs_c, 0)
    base_c = total(i0 == i1, base_l, 1)
    pos = jnp.where(live, 2 * total(hit, base_c, 0) + rho, -1)
    at = to_sub(pos) == iota((MAXB, TAB), 1)
    slot_l = MAXB + total(at, iota((MAXB, TAB), 0) - MAXB, 0)
    col_l = total(at, col_c, 0)
    first = (base_c == iota((LROWS, TAB), 1)) & (pairs_c > 0)
    keep_l = 1 - total(first, 1, 0)
    last_l = jnp.where(pairs_l > 0, base_l + pairs_l - 1, PAIRS)
    return slot_l, col_l, keep_l, last_l


def kernel(
    blocks, rows, cols, count, probes, t_prev, t_cur, accum, coeffs,
    o_next, o_after, o_accum, o_mom,
    mat, vec0, vec1, part, out_buf, in_buf, mom_row, mom_col, mom_own,
    itab, ftab, itab_s, ftab_s,
    mat_sem, tab_sem, ag_s, ag_r, fw_s, fw_r, rs_s, rs_r, ma_s, ma_r, mb_s, mb_r,
):
    r, q = lax.axis_index("row"), lax.axis_index("col")
    x, yl, core = r // 4, (r // 2) % 2, r % 2
    yh, z = q // 8, q % 8

    def row_id(dx, dy, dc=0):
        return ((x + dx) % 4) * 4 + ((yl + dy) % 2) * 2 + (core + dc) % 2

    def col_id(dy, dz):
        return ((yh + dy) % 2) * 8 + (z + dz) % 8

    vec = (vec0, vec1)
    barrier = pltpu.get_barrier_semaphore()
    for i in range(1, 16):
        pl.semaphore_signal(barrier, inc=1, device_id=((r + i) % 16, q), device_id_type=MESH)
        pl.semaphore_signal(barrier, inc=1, device_id=(r, (q + i) % 16), device_id_type=MESH)

    load = pltpu.make_async_copy(blocks, mat.at[pl.ds(0, MAXB)], mat_sem)
    load.start()

    def put_own(step, value):
        own = value.astype(BF16)
        vec[step][2 * r] = own[:, :BS]
        vec[step][2 * r + 1] = own[:, BS:]

    put_own(0, t_cur[...])
    mat[MAXB] = jnp.zeros((BS, BS), BF16)
    part[PAIRS] = jnp.zeros((PROBES, BS), F32)
    slot_l, col_l, keep_l, last_l = tables(rows[...], cols[...], count[0])
    itab[0:1, :] = slot_l
    itab[1:2, :] = col_l
    itab[2:3, 0:BS] = last_l
    ftab[0:1, :] = keep_l.astype(F32)

    pl.semaphore_wait(barrier, 30)

    def remote(src, dst, s_sem, r_sem, dev):
        copy = pltpu.make_async_remote_copy(
            src_ref=src, dst_ref=dst, send_sem=s_sem, recv_sem=r_sem,
            device_id=dev, device_id_type=MESH,
        )
        copy.start()
        return copy

    def gather(step):
        sent = []
        own = vec[step].at[pl.ds(2 * r, 2)]
        mate = (row_id(0, 0, 1), q)
        for n, (dx, dy) in enumerate(ROW_OFFS):
            sent.append(remote(own, own, ag_s.at[step, n], ag_r.at[step, n], (row_id(dx, dy), q)))
        last = len(ROW_OFFS)
        passed = [remote(own, own, fw_s.at[step, last], fw_r.at[step, last], mate)]
        for n in reversed(range(last)):
            dx, dy = ROW_OFFS[n]
            sent[n].wait_recv()
            got = vec[step].at[pl.ds(2 * row_id(4 - dx, dy), 2)]
            passed.append(remote(got, got, fw_s.at[step, n], fw_r.at[step, n], mate))
        for copy in passed:
            copy.wait_recv()
        return sent, passed

    def multiply(step):
        def body(i, acc):
            for u in range(UNROLL):
                n = i * UNROLL + u
                a, b = itab_s[0, 2 * n], itab_s[0, 2 * n + 1]
                c, d = itab_s[1, 2 * n], itab_s[1, 2 * n + 1]
                lhs = jnp.concatenate([vec[step][c], vec[step][d]], axis=1)
                rhs = jnp.concatenate([mat[a], mat[b]], axis=1)
                prod = lax.dot_general(
                    lhs, rhs, (((1,), (1,)), ((), ())), preferred_element_type=F32
                )
                acc = acc * ftab_s[0, n] + prod
                part[n] = acc
            return acc

        lax.fori_loop(0, PAIRS // UNROLL, body, jnp.zeros((PROBES, BS), F32))

    def piece(c):
        lo = part[itab_s[2, 2 * c]]
        hi = part[itab_s[2, 2 * c + 1]]
        return jnp.concatenate([lo, hi], axis=1)

    def scatter(step):
        sent = []
        for n, (dy, dz) in enumerate(COL_OFFS):
            c = col_id(dy, dz)
            out_buf[step, n] = piece(c).astype(BF16)
            sent.append(
                remote(out_buf.at[step, n], in_buf.at[step, n], rs_s.at[step, n], rs_r.at[step, n], (r, c))
            )
        total = piece(q)
        for n in reversed(range(len(COL_OFFS))):
            sent[n].wait_recv()
            total = total + in_buf[step, n].astype(F32)
        return total, sent

    sent0, passed0 = gather(0)
    tab_i = pltpu.make_async_copy(itab, itab_s, tab_sem.at[0])
    tab_f = pltpu.make_async_copy(ftab, ftab_s, tab_sem.at[1])
    tab_i.start()
    tab_f.start()
    tab_i.wait()
    tab_f.wait()
    load.wait()
    multiply(0)
    total, out0 = scatter(0)
    t_next = 2.0 * total - t_prev[...]
    put_own(1, t_next)
    sent1, passed1 = gather(1)
    o_next[...] = t_next
    first = jnp.sum(probes[...] * t_next, axis=1, keepdims=True)
    multiply(1)
    total, out1 = scatter(1)
    t_after = 2.0 * total - t_cur[...]
    o_after[...] = t_after
    o_accum[...] = accum[...] + coeffs[0] * o_next[...] + coeffs[1] * t_after
    second = jnp.sum(probes[...] * t_after, axis=1, keepdims=True)

    diag = iota((PROBES, BS), 0) == iota((PROBES, BS), 1)
    flat = lambda m: jnp.sum(jnp.where(diag, m, 0.0), axis=0, keepdims=True)
    mom_own[0, 0:1, :] = flat(first)
    mom_own[0, 1:2, :] = flat(second)
    copies = []
    for i in range(1, 16):
        dev = ((r + i) % 16, q)
        copies.append(remote(mom_own.at[0], mom_row.at[r], ma_s.at[i], ma_r.at[i], dev))
    mom_row[r] = mom_own[0]
    for copy in copies:
        copy.wait_recv()
    mom_own[1] = jnp.sum(mom_row[...], axis=0)
    more = []
    for i in range(1, 16):
        dev = (r, (q + i) % 16)
        more.append(remote(mom_own.at[1], mom_col.at[q], mb_s.at[i], mb_r.at[i], dev))
    mom_col[q] = mom_own[1]
    for copy in more:
        copy.wait_recv()
    scale = float(LROWS * BS * 16) ** -0.5
    o_mom[...] = jnp.sum(mom_col[...], axis=0)[0:2, 0:PROBES] * scale
    for copy in copies + more + sent0 + passed0 + sent1 + passed1 + out0 + out1:
        copy.wait_send()


def local(blocks, block_rows, block_cols, block_count, probes, t_prev, t_cur, accum, coeffs):
    vmem = pl.BlockSpec(memory_space=pltpu.VMEM)
    smem = pl.BlockSpec(memory_space=pltpu.SMEM)
    width = t_cur.shape[1]
    big = jax.ShapeDtypeStruct((PROBES, width), F32)
    sem = pltpu.SemaphoreType.DMA
    return pl.pallas_call(
        kernel,
        out_shape=(big, big, big, jax.ShapeDtypeStruct((2, PROBES), F32)),
        in_specs=[pl.BlockSpec(memory_space=pl.ANY), vmem, vmem, smem, vmem, vmem, vmem, vmem, smem],
        out_specs=(vmem, vmem, vmem, vmem),
        scratch_shapes=[
            pltpu.VMEM((MAXB + 1, BS, BS), BF16),
            pltpu.VMEM((LROWS, PROBES, BS), BF16),
            pltpu.VMEM((LROWS, PROBES, BS), BF16),
            pltpu.VMEM((PAIRS + 1, PROBES, BS), F32),
            pltpu.VMEM((2, 15, PROBES, width), BF16),
            pltpu.VMEM((2, 15, PROBES, width), BF16),
            pltpu.VMEM((16, 8, BS), F32),
            pltpu.VMEM((16, 8, BS), F32),
            pltpu.VMEM((2, 8, BS), F32),
            pltpu.VMEM((8, TAB), jnp.int32),
            pltpu.VMEM((8, TAB), F32),
            pltpu.SMEM((8, TAB), jnp.int32),
            pltpu.SMEM((8, TAB), F32),
            sem,
            sem((2,)),
            sem((2, 7)), sem((2, 7)), sem((2, 8)), sem((2, 8)),
            sem((2, 15)), sem((2, 15)),
            sem((16,)), sem((16,)), sem((16,)), sem((16,)),
        ],
        compiler_params=pltpu.CompilerParams(
            collective_id=0, has_side_effects=True, vmem_limit_bytes=48 << 20
        ),
    )(
        blocks.reshape(MAXB, BS, BS), block_rows.reshape(1, MAXB), block_cols.reshape(1, MAXB),
        block_count.reshape(1), probes, t_prev, t_cur, accum, coeffs,
    )


def solution(mesh):
    split = P(None, ("row", "col"))
    return jax.shard_map(
        local,
        mesh=mesh,
        in_specs=(
            P("row", "col", None, None, None), P("row", "col", None), P("row", "col", None),
            P("row", "col"), split, split, split, split, P(),
        ),
        out_specs=(split, split, split, P()),
        check_vma=False,
    )
```

time: 567 us -> 82.5 us (0.15)
  waiting for transfers between devices: 346 us -> 0 us
  blocking collectives: 139 us -> 0 us
  Pallas kernels: 0 us -> 73.1 us
  other arithmetic: 39.5 us -> 0 us
  matrix products: 16.6 us -> 0 us
  between operations: 14.8 us -> 1.3 us
    psum x2 -> x0, waiting for transfers between devices: 346 us -> none  [product(): summed = lax.psum(partial_value, 'col')]
    psum x1 -> x0, blocking collectives: 85.2 us -> none  [moment_one(): return lax.psum(local_sum, ('row', 'col'))]
    pallas_call x0 -> x1, Pallas kernels: none -> 73.1 us  [local(): pl.pallas_call(kernel, out_shape=(big, big, big, jax.ShapeDtypeStruct((2,...]
    all_gather x2 -> x0, blocking collectives: 53.9 us -> none  [product(): lax.all_gather(vectors.astype(jnp.bfloat16), 'row', axis=1, tiled=True)]
    scatter-add x8 -> x0, other arithmetic: 17 us -> none  [add_group(): return total.at[:, group_rows, :].add(contrib)]
    dot_general x8 -> x0, matrix products: 16.6 us -> none  [add_group(): jnp.einsum('pgj,gij->pgi', picked, tile_group, preferred_element_type=jnp...]
    and x8 -> x0, other arithmetic: 11.2 us -> none  [add_group(): picked = jnp.take(column_set, group_cols, axis=1)]
    unnamed x14 -> x18, local copies, waits for them, and re-layouts: 0.05 us -> 7.81 us
  transfers between devices with their start and end apart: 2 -> 0, of which waited for: 2 -> 0; matrix products, arithmetic and copies ran while one was open for 0% -> 0% of each run, Pallas kernels for 0% -> 0%
where the time goes in v1:
time: 82.5 us; the launch traced here: 82.2 us
  Pallas kernels  73.1 us (89%)
  local copies, waits for them, and re-layouts  7.81 us (9%)
  between operations  1.3 us (2%)
    pallas_call x1, Pallas kernels, local(): pl.pallas_call(kernel, out_shape=(big, big, big, jax.ShapeDtypeStruct((2,...  73.1 us
    unnamed x18, local copies, waits for them, and re-layouts  7.81 us

profile of v1, /device:TPU:1, one launch (start us, length us, event | category | flops | bytes accessed | tf_op | source)
XLA Modules:
  0.0 82.2 jit_solution(776225282873002395)
XLA Ops:
  1.3 0.0 copy-start
  1.3 0.8 %copy-done = f32[64,256]{1,0:T(8,128)S(1)} copy-done((f32[64,256]{1,0:T(8,128)S(1)}, f32[64,256]{1,0:T(8,128)}, u32[]{:S(2)}) %copy-start) | copy-done | bytes 65560
  2.1 0.0 copy-start.1
  2.1 0.8 %copy-done.1 = f32[64,256]{1,0:T(8,128)S(1)} copy-done((f32[64,256]{1,0:T(8,128)S(1)}, f32[64,256]{1,0:T(8,128)}, u32[]{:S(2)}) %copy-start.1) | copy-done | bytes 65560
  3.0 0.0 copy-start.2
  3.0 0.8 %copy-done.2 = f32[64,256]{1,0:T(8,128)S(1)} copy-done((f32[64,256]{1,0:T(8,128)S(1)}, f32[64,256]{1,0:T(8,128)}, u32[]{:S(2)}) %copy-start.2) | copy-done | bytes 65560
  3.8 0.0 copy-start.3
  3.8 0.8 %copy-done.3 = f32[64,256]{1,0:T(8,128)S(1)} copy-done((f32[64,256]{1,0:T(8,128)S(1)}, f32[64,256]{1,0:T(8,128)}, u32[]{:S(2)}) %copy-start.3) | copy-done | bytes 65560
  4.6 0.0 copy-start.4
  4.6 0.7 copy-done.4
  5.3 0.0 copy-start.5
  5.3 0.7 copy-done.5
  6.0 0.0 copy-start.6
  6.0 0.7 copy-done.6
  6.7 73.1 %shard_map.120 = (f32[64,256]{1,0:T(8,128)S(1)}, f32[64,256]{1,0:T(8,128)S(1)}, f32[64,256]{1,0:T(8,128)S(1)}, f32[2,64]{1,0:T(2,128)S(1)}) custom-call(bf16[256,128,128]{2,1,0:T(8,128)(2,1)} %bitcast.7, s32[1,256]{1,0:T(1,128)S(1)} %bitcast.5, s32[1,256]{1,0:T(1,128)S(1)} %bitcast.6, s32[1]{0:T(128)} %bitcast.4.count, f32[64,256]{1,0:T(8,128)S(1)} %copy-done, ...), custom_call_target="tpu_custom_call" | custom-call | tf_op jit(solution)/shard_map/pallas_call | solution.py:213
  79.8 0.6 copy.18
  80.4 0.6 copy.19
  81.0 0.6 copy.20
  81.7 0.6 copy.21
Async XLA Ops:
  1.3 0.8 %copy-start = (f32[64,256]{1,0:T(8,128)S(1)}, f32[64,256]{1,0:T(8,128)}, u32[]{:S(2)}) copy-start(f32[64,256]{1,0:T(8,128)} %probes.1) | copy-start | bytes 196612
  2.1 0.8 %copy-start.1 = (f32[64,256]{1,0:T(8,128)S(1)}, f32[64,256]{1,0:T(8,128)}, u32[]{:S(2)}) copy-start(f32[64,256]{1,0:T(8,128)} %t_prev.1) | copy-start | bytes 196612
  3.0 0.8 %copy-start.2 = (f32[64,256]{1,0:T(8,128)S(1)}, f32[64,256]{1,0:T(8,128)}, u32[]{:S(2)}) copy-start(f32[64,256]{1,0:T(8,128)} %t_cur.1) | copy-start | bytes 196612
  3.8 0.8 %copy-start.3 = (f32[64,256]{1,0:T(8,128)S(1)}, f32[64,256]{1,0:T(8,128)}, u32[]{:S(2)}) copy-start(f32[64,256]{1,0:T(8,128)} %accum.1) | copy-start | bytes 196612
  4.6 0.7 copy-start.4
  5.3 0.7 copy-start.5
  6.0 0.7 copy-start.6

commit v2 on v1

v2 whole, which is shorter than its diff:
```python
import jax
import jax.numpy as jnp
from jax import lax
from jax.experimental import pallas as pl
from jax.experimental.pallas import tpu as pltpu
from jax.sharding import PartitionSpec as P

MESH = pl.DeviceIdType.MESH
F32 = jnp.float32
BF16 = jnp.bfloat16
BS = 128
PROBES = 64
MAXB = 256
LROWS = 32
PAIRS = 144
TAB = 384
UNROLL = 24
ROW_OFFS = ((2, 1), (2, 0), (1, 1), (3, 1), (1, 0), (3, 0), (0, 1))
COL_OFFS = (
    (1, 4), (0, 4), (1, 3), (1, 5), (0, 3), (0, 5), (1, 2), (1, 6),
    (0, 2), (0, 6), (1, 1), (1, 7), (0, 1), (0, 7), (1, 0),
)
PACK = 8


def iota(shape, axis):
    return lax.broadcasted_iota(jnp.int32, shape, axis)


def to_sub(row):
    n = row.shape[1]
    eye = iota((n, n), 0) == iota((n, n), 1)
    return jnp.sum(jnp.where(eye, row, 0), axis=1, keepdims=True)


def tables(rows, cols, count):
    total = lambda mask, value, axis: jnp.sum(jnp.where(mask, value, 0), axis=axis, keepdims=True)
    live = iota((1, MAXB), 1) < count
    row_l = jnp.where(live, rows, 1000)
    row_c, col_c = to_sub(row_l), to_sub(cols)
    rho = total((row_c == row_l) & (col_c < cols), 1, 0)
    hit = iota((LROWS, MAXB), 0) == row_l
    pairs_c = (total(hit, 1, 1) + 1) >> 1
    i0, i1 = iota((LROWS, BS), 0), iota((LROWS, BS), 1)
    base_l = total(i0 < i1, pairs_c, 0)
    pairs_l = total(i0 == i1, pairs_c, 0)
    base_c = total(i0 == i1, base_l, 1)
    pos = jnp.where(live, 2 * total(hit, base_c, 0) + rho, -1)
    at = to_sub(pos) == iota((MAXB, TAB), 1)
    slot_l = MAXB + total(at, iota((MAXB, TAB), 0) - MAXB, 0)
    col_l = total(at, col_c, 0)
    first = (base_c == iota((LROWS, TAB), 1)) & (pairs_c > 0)
    keep_l = 1 - total(first, 1, 0)
    last_l = jnp.where(pairs_l > 0, base_l + pairs_l - 1, PAIRS)
    return slot_l, col_l, keep_l, last_l


def kernel(
    blocks, rows_h, cols_h, count_h, probes_h, t_prev_h, t_cur_h,
    o_first, o_second, o_mom,
    mat, packed, vec0, vec1, part, out_buf, in_buf, probes_all, mom_col, mom_row, mom_own,
    rows, cols, count, probes, t_prev, t_cur,
    itab, ftab, itab_s, ftab_s,
    in_sem, tab_sem, ag_s, ag_r, fw_s, fw_r, rs_s, rs_r, pr_s, pr_r, ma_s, ma_r, mb_s, mb_r,
    near_sem, mid_sem, far_sem,
):
    r, q = lax.axis_index("row"), lax.axis_index("col")
    x, yl, core = r // 4, (r // 2) % 2, r % 2
    yh, z = q // 8, q % 8
    vec = (vec0, vec1)

    def row_id(dx, dy, dc=0):
        return ((x + dx) % 4) * 4 + ((yl + dy) % 2) * 2 + (core + dc) % 2

    def col_id(dy, dz):
        return ((yh + dy) % 2) * 8 + (z + dz) % 8

    def signal(sem, dev):
        pl.semaphore_signal(sem, inc=1, device_id=dev, device_id_type=MESH)

    def remote(src, dst, s_sem, r_sem, dev):
        copy = pltpu.make_async_remote_copy(
            src_ref=src, dst_ref=dst, send_sem=s_sem, recv_sem=r_sem,
            device_id=dev, device_id_type=MESH,
        )
        copy.start()
        return copy

    barrier = pltpu.get_barrier_semaphore()
    close = [(r, col_id(0, 1)), (r, col_id(0, 7)), (r, col_id(1, 0))]
    for dev in close + [((r + i) % 16, q) for i in range(1, 16)]:
        signal(barrier, dev)

    loads = []
    for n, (src, dst) in enumerate((
        (t_cur_h, t_cur), (rows_h, rows), (cols_h, cols), (count_h, count),
        (blocks, mat.at[pl.ds(0, MAXB)]), (probes_h, probes), (t_prev_h, t_prev),
    )):
        copy = pltpu.make_async_copy(src, dst, in_sem.at[n])
        copy.start()
        loads.append(copy)

    def put_own(step, value):
        own = value.astype(BF16)
        vec[step][2 * r] = own[:, :BS]
        vec[step][2 * r + 1] = own[:, BS:]

    def gather_start(step):
        own = vec[step].at[pl.ds(2 * r, 2)]
        mate = (row_id(0, 0, 1), q)
        sent = []
        for n, (dx, dy) in enumerate(ROW_OFFS):
            sent.append(remote(own, own, ag_s.at[step, n], ag_r.at[step, n], (row_id(dx, dy), q)))
        last = len(ROW_OFFS)
        passed = [remote(own, own, fw_s.at[step, last], fw_r.at[step, last], mate)]
        return sent, passed

    def pass_on(step, sent, passed, which):
        mate = (row_id(0, 0, 1), q)
        for n in which:
            dx, dy = ROW_OFFS[n]
            sent[n].wait_recv()
            got = vec[step].at[pl.ds(2 * row_id(4 - dx, dy), 2)]
            passed.append(remote(got, got, fw_s.at[step, n], fw_r.at[step, n], mate))

    def share_probes(offs):
        sent = []
        for dy, dz in offs:
            n = dy * 8 + dz
            sent.append(remote(probes_all.at[q], probes_all.at[q], pr_s.at[n], pr_r.at[n], (r, col_id(dy, dz))))
        return sent

    def pack(lo, hi):
        def body(i, _):
            for u in range(PACK):
                n = i * PACK + u
                packed[n] = mat[itab_s[0, n]].T
            return 0

        lax.fori_loop(lo // PACK, hi // PACK, body, 0)

    def multiply(step):
        def body(i, acc):
            for u in range(UNROLL):
                n = i * UNROLL + u
                c, d = itab_s[1, 2 * n], itab_s[1, 2 * n + 1]
                lhs = jnp.concatenate([vec[step][c], vec[step][d]], axis=1)
                rhs = packed[pl.ds(2 * n, 2)].reshape(2 * BS, BS)
                acc = acc * ftab_s[0, n] + jnp.dot(lhs, rhs, preferred_element_type=F32)
                part[n] = acc
            return acc

        lax.fori_loop(0, PAIRS // UNROLL, body, jnp.zeros((PROBES, BS), F32))

    def piece(c):
        lo = part[itab_s[2, 2 * c]]
        hi = part[itab_s[2, 2 * c + 1]]
        return jnp.concatenate([lo, hi], axis=1)

    def scatter_start(step, offs):
        sent = []
        for dy, dz in offs:
            n, c = COL_OFFS.index((dy, dz)), col_id(dy, dz)
            out_buf[step, n] = piece(c).astype(BF16)
            sent.append(
                remote(out_buf.at[step, n], in_buf.at[step, n], rs_s.at[step, n], rs_r.at[step, n], (r, c))
            )
        return sent

    def scatter_sum(step, sent):
        total = piece(q)
        for n in reversed(range(len(COL_OFFS))):
            sent[n].wait_recv()
            total = total + in_buf[step, n].astype(F32)
        return total

    loads[0].wait()
    put_own(0, t_cur[...])
    pl.semaphore_wait(barrier, 18)
    sent0, passed0 = gather_start(0)
    for dev in close:
        signal(near_sem, dev)

    mat[MAXB] = jnp.zeros((BS, BS), BF16)
    part[PAIRS] = jnp.zeros((PROBES, BS), F32)
    for copy in loads[1:4]:
        copy.wait()
    slot_l, col_l, keep_l, last_l = tables(rows[...], cols[...], count[...])
    itab[0:1, :] = slot_l
    itab[1:2, :] = col_l
    itab[2:3, 0:BS] = last_l
    ftab[0:1, :] = keep_l.astype(F32)
    for copy in loads[4:]:
        copy.wait()
    probes_all[q] = probes[...].astype(BF16)
    pl.semaphore_wait(near_sem, 3)
    for dz in (2, 6):
        signal(mid_sem, (r, col_id(0, dz)))
    tab_i = pltpu.make_async_copy(itab, itab_s, tab_sem.at[0])
    tab_f = pltpu.make_async_copy(ftab, ftab_s, tab_sem.at[1])
    tab_i.start()
    tab_f.start()
    tab_i.wait()
    tab_f.wait()
    pack(0, 96)
    pass_on(0, sent0, passed0, (6, 5, 4))
    pl.semaphore_wait(mid_sem, 2)
    signal(far_sem, (r, col_id(1, 0)))
    shared = share_probes([(0, dz) for dz in (4, 3, 5, 2, 6, 1, 7)])
    pack(96, 192)
    pass_on(0, sent0, passed0, (3, 2))
    pack(192, 288)
    pass_on(0, sent0, passed0, (1, 0))
    for copy in passed0:
        copy.wait_recv()
    multiply(0)
    pl.semaphore_wait(far_sem, 1)
    out0 = scatter_start(0, COL_OFFS)
    total = scatter_sum(0, out0)
    t_next = 2.0 * total - t_prev[...]
    put_own(1, t_next)
    sent1, passed1 = gather_start(1)
    shared += share_probes([(1, dz) for dz in (4, 3, 5, 2, 6, 1, 7, 0)])
    o_first[...] = total
    first = jnp.sum(probes[...] * t_next, axis=1, keepdims=True)
    before = jnp.sum(probes[...] * t_cur[...], axis=1, keepdims=True)
    pass_on(1, sent1, passed1, (6, 5, 4, 3, 2, 1, 0))
    for copy in passed1:
        copy.wait_recv()
    multiply(1)
    out1 = scatter_start(1, COL_OFFS[:4])

    for copy in shared:
        copy.wait_recv()

    def weigh(c, acc):
        return acc + probes_all[c].astype(F32) * piece(c)

    held = lax.fori_loop(0, 16, weigh, jnp.zeros((PROBES, 2 * BS), F32))
    second = 2.0 * jnp.sum(held, axis=1, keepdims=True) - before
    i0, i1 = iota((PROBES, BS), 0), iota((PROBES, BS), 1)
    both = jnp.where(i0 == i1, first, 0.0) + jnp.where(i0 + PROBES == i1, second, 0.0)
    mine = jnp.sum(both, axis=0, keepdims=True)
    mom_own[0] = mine
    mom_col[q] = mine
    copies = []
    for n, (dy, dz) in enumerate(COL_OFFS):
        dev = (r, col_id(dy, dz))
        copies.append(remote(mom_own.at[0], mom_col.at[q], ma_s.at[n], ma_r.at[n], dev))
    out1 += scatter_start(1, COL_OFFS[4:])
    for copy in copies:
        copy.wait_recv()
    mine = jnp.sum(mom_col[...], axis=0)
    mom_own[1] = mine
    mom_row[r] = mine
    more = []
    for i in range(1, 16):
        dev = ((r + i) % 16, q)
        more.append(remote(mom_own.at[1], mom_row.at[r], mb_s.at[i], mb_r.at[i], dev))
    o_second[...] = scatter_sum(1, out1)
    for copy in more:
        copy.wait_recv()
    scale = float(LROWS * BS * 16) ** -0.5
    summed = jnp.sum(mom_row[...], axis=0) * scale
    o_mom[0:1, :] = summed[:, :PROBES]
    o_mom[1:2, :] = summed[:, PROBES:]
    for copy in copies + more + shared + sent0 + passed0 + sent1 + passed1 + out0 + out1:
        copy.wait_send()


def local(blocks, block_rows, block_cols, block_count, probes, t_prev, t_cur, accum, coeffs):
    vmem = pl.BlockSpec(memory_space=pltpu.VMEM)
    hbm = pl.BlockSpec(memory_space=pltpu.HBM)
    width = t_cur.shape[1]
    big = jax.ShapeDtypeStruct((PROBES, width), F32)
    sem = pltpu.SemaphoreType.DMA
    regular = pltpu.SemaphoreType.REGULAR
    first, second, moments = pl.pallas_call(
        kernel,
        out_shape=(big, big, jax.ShapeDtypeStruct((2, PROBES), F32)),
        in_specs=[hbm] * 7,
        out_specs=(vmem, vmem, vmem),
        scratch_shapes=[
            pltpu.VMEM((MAXB + 1, BS, BS), BF16),
            pltpu.VMEM((2 * PAIRS, BS, BS), BF16),
            pltpu.VMEM((LROWS, PROBES, BS), BF16),
            pltpu.VMEM((LROWS, PROBES, BS), BF16),
            pltpu.VMEM((PAIRS + 1, PROBES, BS), F32),
            pltpu.VMEM((2, 15, PROBES, width), BF16),
            pltpu.VMEM((2, 15, PROBES, width), BF16),
            pltpu.VMEM((16, PROBES, width), BF16),
            pltpu.VMEM((16, 1, BS), F32),
            pltpu.VMEM((16, 1, BS), F32),
            pltpu.VMEM((2, 1, BS), F32),
            pltpu.VMEM((1, MAXB), jnp.int32),
            pltpu.VMEM((1, MAXB), jnp.int32),
            pltpu.VMEM((1, 1), jnp.int32),
            pltpu.VMEM((PROBES, width), F32),
            pltpu.VMEM((PROBES, width), F32),
            pltpu.VMEM((PROBES, width), F32),
            pltpu.VMEM((8, TAB), jnp.int32),
            pltpu.VMEM((8, TAB), F32),
            pltpu.SMEM((8, TAB), jnp.int32),
            pltpu.SMEM((8, TAB), F32),
            sem((7,)),
            sem((2,)),
            sem((2, 7)), sem((2, 7)), sem((2, 8)), sem((2, 8)),
            sem((2, 15)), sem((2, 15)), sem((16,)), sem((16,)),
            sem((16,)), sem((16,)), sem((16,)), sem((16,)),
            regular, regular, regular,
        ],
        compiler_params=pltpu.CompilerParams(
            collective_id=0, has_side_effects=True, vmem_limit_bytes=60 << 20
        ),
    )(
        blocks.reshape(MAXB, BS, BS), block_rows.reshape(1, MAXB), block_cols.reshape(1, MAXB),
        block_count, probes, t_prev, t_cur,
    )
    t_next = 2.0 * first - t_prev
    t_after = 2.0 * second - t_cur
    accum_out = accum + coeffs[0] * t_next + coeffs[1] * t_after
    return t_next, t_after, accum_out, moments


def solution(mesh):
    split = P(None, ("row", "col"))
    return jax.shard_map(
        local,
        mesh=mesh,
        in_specs=(
            P("row", "col", None, None, None), P("row", "col", None), P("row", "col", None),
            P("row", "col"), split, split, split, split, P(),
        ),
        out_specs=(split, split, split, P()),
        check_vma=False,
    )
```

time: 82.5 us -> 72.5 us (0.88)
  Pallas kernels: 73.1 us -> 65.5 us
  local copies, waits for them, and re-layouts: 7.81 us -> 2.56 us
  other arithmetic: 0 us -> 2.83 us
    pallas_call x1, Pallas kernels: 73.1 us -> 65.5 us  [local(): pl.pallas_call(kernel, out_shape=(big, big, jax.ShapeDtypeStruct((2, PROB...]
    unnamed x18 -> x7, local copies, waits for them, and re-layouts: 7.81 us -> 1.21 us
    add x0 -> x1, other arithmetic: none -> 2.83 us  [local(): accum_out = accum + coeffs[0] * t_next + coeffs[1] * t_after]
    slice x0 -> x1, local copies, waits for them, and re-layouts: none -> 1.35 us  [local(): accum_out = accum + coeffs[0] * t_next + coeffs[1] * t_after]
where the time goes in v2:
time: 72.5 us; the launch traced here: 72.2 us
  Pallas kernels  65.5 us (90%)
  other arithmetic  2.83 us (4%)
  local copies, waits for them, and re-layouts  2.56 us (4%)
  between operations  1.37 us (2%)
    pallas_call x1, Pallas kernels, local(): pl.pallas_call(kernel, out_shape=(big, big, jax.ShapeDtypeStruct((2, PROB...  65.5 us
    add x1, other arithmetic, local(): accum_out = accum + coeffs[0] * t_next + coeffs[1] * t_after  2.83 us

profile of v2, /device:TPU:1, one launch (start us, length us, event | category | flops | bytes accessed | tf_op | source)
XLA Modules:
  0.0 72.2 jit_solution(884206727496655999)
XLA Ops:
  0.6 0.0 copy-start
  0.6 0.0 copy-start.1
  0.7 0.0 copy-start.2
  1.3 1.3 %fusion = (f32[1]{0:T(128)}, f32[1]{0:T(128)}) fusion(f32[2]{0:T(128)} %param.17), kind=kLoop, calls=%fused_computation.3 | loop fusion | bytes 16 | tf_op jit(solution)/shard_map/slice | solution.py:321
  2.7 65.5 %shard_map.120 = (f32[64,256]{1,0:T(8,128)}, f32[64,256]{1,0:T(8,128)}, f32[2,64]{1,0:T(2,128)}) custom-call(bf16[256,128,128]{2,1,0:T(8,128)(2,1)} %bitcast.5, s32[1,256]{1,0:T(1,128)} %bitcast.6, s32[1,256]{1,0:T(1,128)} %bitcast.7, s32[1,1]{1,0:T(1,128)S(6)} %copy.14.count_h, f32[64,256]{1,0:T(8,128)} %probes_h.1, f32[64,256]{1,0:T(8,128)} %t_prev_h.1, ...), custom_call_target="tpu_custom_call" | custom-call | tf_op jit(solution)/shard_map/pallas_call | solution.py:278
  68.2 0.0 copy-done
  68.2 0.0 copy-done.1
  68.2 0.0 copy-done.2
  68.2 2.8 %multiply_add_fusion = (f32[64,256]{1,0:T(8,128)}, f32[64,256]{1,0:T(8,128)}, f32[64,256]{1,0:T(8,128)}) fusion(f32[64,256]{1,0:T(8,128)S(1)} %copy-done.2, f32[]{:T(128)} %bitcast.4, f32[]{:T(128)} %bitcast.3, f32[64,256]{1,0:T(8,128)S(1)} %copy-done, f32[64,256]{1,0:T(8,128)} %get-tuple-element.8, f32[64,256]{1,0:T(8,128)S(1)} %copy-done.1, ...), kind=kLoop, calls=%fused_computation | loop fusion | flops 131072 | bytes 524296 | tf_op jit(solution)/shard_map/add | solution.py:321
  71.1 1.2 %copy.15 = f32[2,64]{1,0:T(2,128)} copy(f32[2,64]{1,0:T(2,128)} %get-tuple-element.22) | data formatting | bytes 1024
Async XLA Ops:
  0.6 67.6 %copy-start = (f32[64,256]{1,0:T(8,128)S(1)}, f32[64,256]{1,0:T(8,128)}, u32[]{:S(2)}) copy-start(f32[64,256]{1,0:T(8,128)} %t_cur_h.1) | copy-start | bytes 196612
  0.6 67.6 %copy-start.1 = (f32[64,256]{1,0:T(8,128)S(1)}, f32[64,256]{1,0:T(8,128)}, u32[]{:S(2)}) copy-start(f32[64,256]{1,0:T(8,128)} %t_prev_h.1) | copy-start | bytes 196612
  0.7 67.6 %copy-start.2 = (f32[64,256]{1,0:T(8,128)S(1)}, f32[64,256]{1,0:T(8,128)}, u32[]{:S(2)}) copy-start(f32[64,256]{1,0:T(8,128)} %param.16) | copy-start | bytes 196612
